TPU v7x, 256 devices: a whole 4x4x8 slice. The times are simulated.
256 devices in a mesh: cuts: 8 (over y, core), dom: 32 (over z, x).
Axes of the slice: x: 4, y: 4, z: 8, core: 2. Of those that a mesh axis runs over, the one named last changes fastest.
Arguments:
- feats: bfloat16 [65536, 4096], P('dom', 'cuts'), may hold values from -6 to 6
- adjacency: bfloat16 [2048, 128, 128], P('dom'), may hold values from 0 to 0.024658203
- blk_dst: int32 [2048], P('dom'), may hold values from 0 to 31
- blk_src: int32 [2048], P('dom'), may hold values from 0 to 15
- blk_count: int32 [32], P('dom'), may hold values from 1 to 64, as said below
- nbr_ids: int32 [4096, 8], P('dom'), may hold values from 0 to 4095
- edge_types: int32 [4096, 8], P('dom'), may hold values from 0 to 3
- w_first: bfloat16 [4096, 128], P('cuts'), may hold values from -0.09375 to 0.09375
- w_edge: bfloat16 [128, 512], replicated, may hold values from -0.1875 to 0.1875
- w_gate_in: bfloat16 [128, 384], replicated, may hold values from -0.5 to 0.5
- w_gate_state: bfloat16 [128, 256], replicated, may hold values from -0.5 to 0.5
- w_cand: bfloat16 [128, 128], replicated, may hold values from -0.5 to 0.5
- out_grad: bfloat16 [4096, 128], P('dom'), may hold values from -0.5 to 0.5
Outputs:
- new_state: bfloat16 [4096, 128], P('dom')
- w_first_grad: float32 [4096, 128], P(('cuts', 'dom'))
Inputs may be any that keep to these rules, and one draw needn't show every extreme that they name: `blk_count`: slot b counts for partition b // 64 only if b mod 64 is below this count; the other slots are padding; some partition has all 64 slots live. `blk_dst`: a destination block number. `blk_src`: a source block number within the partition.
All inputs are finite; a program needn't handle non-finite values.
Results may differ from a plain program's by a relative error of at most 0.0075.
Values may be sent and summed in bfloat16 or wider, within the bound.
No kernel may reach another device: no remote copies, remote signals or barrier semaphores. Data moves between devices by JAX's collectives and lax.ppermute only.
A program may use at most 64 MiB of HBM per device.

v0:
```python
import math
import jax
import jax.numpy as jnp
from jax import lax
from jax.sharding import PartitionSpec as P


def edge_messages(states, nbr_ids, edge_types, w_edge):
    row_count, fanout = nbr_ids.shape
    hidden = states.shape[1]
    num_types = w_edge.shape[1] // hidden
    picked = states[nbr_ids.reshape(-1)]
    projected = jnp.dot(picked, w_edge, preferred_element_type=jnp.float32).reshape(
        row_count, fanout, num_types, hidden
    )
    one_hot = (
        edge_types[:, :, None] == jnp.arange(num_types, dtype=jnp.int32)[None, None, :]
    ).astype(jnp.float32)
    return jnp.sum(projected * one_hot[:, :, :, None], axis=(1, 2))


def edge_backward(message_grad, nbr_ids, edge_types, w_edge):
    row_count, fanout = nbr_ids.shape
    hidden = message_grad.shape[1]
    num_types = w_edge.shape[1] // hidden
    w_back = (
        w_edge.reshape(hidden, num_types, hidden)
        .transpose(2, 1, 0)
        .reshape(hidden, num_types * hidden)
    )
    per_type = jnp.dot(message_grad, w_back, preferred_element_type=jnp.float32).reshape(
        row_count, 1, num_types, hidden
    )
    one_hot = (
        edge_types[:, :, None] == jnp.arange(num_types, dtype=jnp.int32)[None, None, :]
    ).astype(jnp.float32)
    return jnp.sum(per_type * one_hot[:, :, :, None], axis=2)


def gated_update(message, states, out_grad, w_gate_in, w_gate_state, w_cand):
    hidden = states.shape[1]
    message_in = message.astype(jnp.bfloat16)
    gate_in = jnp.dot(message_in, w_gate_in, preferred_element_type=jnp.float32)
    gate_state = jnp.dot(states, w_gate_state, preferred_element_type=jnp.float32)
    state_value = states.astype(jnp.float32)
    update = jax.nn.sigmoid(gate_in[:, :hidden] + gate_state[:, :hidden])
    reset = jax.nn.sigmoid(gate_in[:, hidden : 2 * hidden] + gate_state[:, hidden:])
    reset_state = (reset * state_value).astype(jnp.bfloat16)
    candidate = jnp.tanh(
        gate_in[:, 2 * hidden :] + jnp.dot(reset_state, w_cand, preferred_element_type=jnp.float32)
    )
    new_state = ((1.0 - update) * candidate + update * state_value).astype(jnp.bfloat16)
    out_value = out_grad.astype(jnp.float32)
    cand_pre = out_value * (1.0 - update) * (1.0 - candidate * candidate)
    update_pre = out_value * (state_value - candidate) * update * (1.0 - update)
    cand_grad = cand_pre.astype(jnp.bfloat16)
    reset_grad_in = jnp.dot(cand_grad, w_cand.T, preferred_element_type=jnp.float32)
    reset_pre = reset_grad_in * state_value * reset * (1.0 - reset)
    gate_grads = jnp.concatenate([update_pre, reset_pre, cand_pre], axis=1).astype(jnp.bfloat16)
    message_grad = jnp.dot(gate_grads, w_gate_in.T, preferred_element_type=jnp.float32).astype(
        jnp.bfloat16
    )
    state_grad = (
        out_value * update
        + reset_grad_in * reset
        + jnp.dot(gate_grads[:, : 2 * hidden], w_gate_state.T, preferred_element_type=jnp.float32)
    )
    return (new_state, message_grad, state_grad)


def rows_in_window(flat_contrib, flat_targets, rows_wanted):
    inside = (flat_targets >= 0) & (flat_targets < rows_wanted)
    summed = jax.ops.segment_sum(
        jnp.where(inside[:, None], flat_contrib, 0.0),
        jnp.where(inside, flat_targets, rows_wanted),
        num_segments=rows_wanted + 1,
    )
    return summed[:rows_wanted]


def body(
    feats,
    adjacency,
    blk_dst,
    blk_src,
    blk_count,
    nbr_ids,
    edge_types,
    w_first,
    w_edge,
    w_gate_in,
    w_gate_state,
    w_cand,
    out_grad,
):
    block_count = adjacency.shape[0]
    block_rows = adjacency.shape[1]
    feat_cols = feats.shape[1]
    hidden = w_first.shape[1]
    row_count = out_grad.shape[0]
    domains = lax.axis_size("dom")
    total_rows = row_count * domains
    feat_tiles = feats.reshape(-1, block_rows, feat_cols)
    live_mask = jnp.arange(block_count, dtype=jnp.int32) < blk_count[0]
    group_size = math.gcd(block_count, 16)
    groups = block_count // group_size

    def one_group(group):
        adj_group, src_group, live_group = group
        src_rows = feat_tiles[src_group]
        aggregated = jnp.einsum(
            "bij,bjf->bif", adj_group, src_rows, preferred_element_type=jnp.float32
        ).astype(jnp.bfloat16)
        projected = jnp.einsum(
            "bif,fh->bih", aggregated, w_first, preferred_element_type=jnp.float32
        )
        return (aggregated, jnp.where(live_group[:, None, None], projected, 0.0))

    aggregated, projected = lax.map(
        one_group,
        (
            adjacency.reshape(groups, group_size, block_rows, block_rows),
            blk_src.reshape(groups, group_size),
            live_mask.reshape(groups, group_size),
        ),
    )
    aggregated = aggregated.reshape(block_count, block_rows, feat_cols)
    projected = projected.reshape(block_count, block_rows, hidden)
    partial_value = jax.ops.segment_sum(
        projected, blk_dst, num_segments=total_rows // block_rows
    ).reshape(total_rows, hidden)
    owned = lax.psum_scatter(partial_value, "dom", scatter_dimension=0, tiled=True)
    first = lax.psum(owned, "cuts")
    state_exact = jnp.tanh(first)
    states = state_exact.astype(jnp.bfloat16)
    all_states = lax.all_gather(states, "dom", axis=0, tiled=True)
    message = edge_messages(all_states, nbr_ids, edge_types, w_edge)
    new_state, message_grad, state_grad = gated_update(
        message, states, out_grad, w_gate_in, w_gate_state, w_cand
    )
    contrib = edge_backward(message_grad, nbr_ids, edge_types, w_edge)
    flat_contrib = contrib.reshape(-1, hidden)
    flat_targets = nbr_ids.reshape(-1)
    state_grad = state_grad + lax.psum_scatter(
        rows_in_window(flat_contrib, flat_targets, lax.axis_size("dom") * row_count),
        "dom",
        scatter_dimension=0,
        tiled=True,
    )
    first_grad = (state_grad * (1.0 - state_exact * state_exact)).astype(jnp.bfloat16)
    all_grads = lax.all_gather(first_grad, "dom", axis=0, tiled=True)
    picked_grads = jnp.where(
        live_mask[:, None, None],
        all_grads.reshape(-1, block_rows, hidden)[blk_dst],
        jnp.zeros((), jnp.bfloat16),
    )
    w_first_grad = lax.psum_scatter(
        jnp.einsum("bif,bih->fh", aggregated, picked_grads, preferred_element_type=jnp.float32),
        "dom",
        scatter_dimension=0,
        tiled=True,
    )
    return (new_state, w_first_grad)


def solution(mesh):
    return jax.shard_map(
        body,
        mesh=mesh,
        in_specs=(
            P("dom", "cuts"),
            P("dom", None, None),
            P("dom"),
            P("dom"),
            P("dom"),
            P("dom", None),
            P("dom", None),
            P("cuts", None),
            P(),
            P(),
            P(),
            P(),
            P("dom", None),
        ),
        out_specs=(P("dom", None), P(("cuts", "dom"), None)),
        check_vma=False,
    )
```

profile of v0, /device:TPU:8, one launch (start us, length us, event | category | flops | bytes accessed | tf_op | source)
XLA Modules:
  0.0 952.8 jit_solution(16278091829357326232)
XLA Ops:
  7.9 0.7 reshape.160
  8.6 28.6 %while.12 = (s32[]{:T(128)}, bf16[4,16,128,512]{3,2,1,0:T(8,128)(2,1)}, f32[4,16,128,128]{3,2,1,0:T(8,128)}, bf16[4,16,128,128]{3,2,1,0:T(8,128)(2,1)}, s32[4,16...) while((s32[]{:T(128)}, ...), condition=%wide.region_1.2_spmd, body=%wide.region_0.1_spmd.sunk | while | flops 538182720 | bytes 14817201 | solution.py:119
  8.7 2.3 gather_fusion
  11.0 3.1 bitcast_dynamic-update-slice_fusion.2
  14.1 1.8 fusion.95
  15.9 2.3 gather_fusion
  18.1 3.1 bitcast_dynamic-update-slice_fusion.2
  21.3 1.7 fusion.95
  23.0 2.3 gather_fusion
  25.2 3.1 bitcast_dynamic-update-slice_fusion.2
  28.4 1.7 fusion.95
  30.1 2.3 gather_fusion
  32.4 3.1 bitcast_dynamic-update-slice_fusion.2
  35.5 1.7 fusion.95
  37.9 8.8 scatter_fusion
  46.7 1.3 copy-done.1
  48.1 221.8 %reduce-scatter.4.cloned.1.call-done = f32[128,128]{1,0:T(8,128)} async-done(((f32[4096,128]{1,0:T(8,128)}), f32[128,128]{1,0:T(8,128)}) %reduce-scatter.4.cloned.1.call-update) | async-done | bytes 65552 | tf_op jit(solution)/shard_map/reduce_scatter | solution.py:132
  270.0 63.2 %all-reduce.2.cloned.1.call-done = f32[128,128]{1,0:T(8,128)} async-done(((f32[128,128]{1,0:T(8,128)}), f32[128,128]{1,0:T(8,128)}) %all-reduce.2.cloned.1.call-update) | async-done | bytes 65552 | tf_op jit(solution)/shard_map/psum | solution.py:133
  333.1 1.5 tanh_convert_fusion
  335.6 0.9 fusion.70
  336.5 77.3 %all-gather.3.cloned.1.call-done = bf16[4096,128]{1,0:T(8,128)(2,1)} async-done(((bf16[128,128]{1,0:T(8,128)(2,1)}), bf16[4096,128]{1,0:T(8,128)(2,1)}) %all-gather.3.cloned.1.call-update) | async-done | bytes 1048592 | tf_op jit(solution)/shard_map/all_gather | solution.py:136
  413.8 4.2 gather_fusion.1
  418.1 0.7 fusion.8
  420.5 0.8 multiply_reduce_fusion
  421.2 7.1 scatter_custom_fusion.1
  428.3 1.5 slice.37
  429.9 216.2 %reduce-scatter.6.cloned.1.call-done = f32[128,128]{1,0:T(8,128)} async-done(((f32[4096,128]{1,0:T(8,128)}), f32[128,128]{1,0:T(8,128)}) %reduce-scatter.6.cloned.1.call-update) | async-done | bytes 65552 | tf_op jit(solution)/shard_map/reduce_scatter | solution.py:144
  646.1 1.6 fusion.18
  647.9 75.4 %all-gather.5.cloned.1.call-done = bf16[4096,128]{1,0:T(8,128)(2,1)} async-done(((bf16[128,128]{1,0:T(8,128)(2,1)}), bf16[4096,128]{1,0:T(8,128)(2,1)}) %all-gather.5.cloned.1.call-update) | async-done | bytes 1048592 | tf_op jit(solution)/shard_map/all_gather | solution.py:151
  723.2 2.2 gather_fusion.2
  725.4 6.7 fusion.12
  732.2 213.7 %reduce-scatter.8.cloned.1.call-done = f32[16,128]{1,0:T(8,128)} async-done(((f32[512,128]{1,0:T(8,128)}), f32[16,128]{1,0:T(8,128)}) %reduce-scatter.8.cloned.1.call-update) | async-done | bytes 8208 | tf_op jit(solution)/shard_map/reduce_scatter | solution.py:157
  (77 shorter events, 3.7 us)
Async XLA Ops:
  7.2 411.6 %copy-start = (bf16[128,384]{1,0:T(8,128)(2,1)S(1)}, bf16[128,384]{1,0:T(8,128)(2,1)}, u32[]{:S(2)}) copy-start(bf16[128,384]{1,0:T(8,128)(2,1)} %param.24) | copy-start | bytes 294916
  7.2 262.7 %reduce-scatter.4.cloned.1.call-start = ((), (), s32[]{:S(2)}) async-start(), calls=%async_computation.3 | async-start | bytes 2162688 | tf_op jit(solution)/shard_map/reduce_scatter | solution.py:132
  10.9 3.1 copy-start.2
  18.1 3.1 copy-start.2
  25.2 3.1 copy-start.2
  32.4 3.1 copy-start.2
  37.2 0.7 copy-start.10
  46.7 1.4 copy-start.1
  46.7 288.0 %copy-start.8 = (s32[128,8]{0,1:T(8,128)S(1)}, s32[128,8]{0,1:T(8,128)}, u32[]{:S(2)}) copy-start(s32[128,8]{0,1:T(8,128)} %param.20) | copy-start | bytes 12292
  46.7 288.2 %copy-start.9 = (s32[128,8]{0,1:T(8,128)S(1)}, s32[128,8]{0,1:T(8,128)}, u32[]{:S(2)}) copy-start(s32[128,8]{0,1:T(8,128)} %param.21) | copy-start | bytes 12292
  46.7 288.3 %copy-start.5 = (bf16[128,512]{1,0:T(8,128)(2,1)S(1)}, bf16[128,512]{1,0:T(8,128)(2,1)}, u32[]{:S(2)}) copy-start(bf16[128,512]{1,0:T(8,128)(2,1)} %param.23) | copy-start | bytes 393220
  46.7 288.9 %copy-start.6 = (bf16[128,256]{1,0:T(8,128)(2,1)S(1)}, bf16[128,256]{1,0:T(8,128)(2,1)}, u32[]{:S(2)}) copy-start(bf16[128,256]{1,0:T(8,128)(2,1)} %param.25) | copy-start | bytes 196612
  48.1 285.1 %all-reduce.2.cloned.1.call-start = ((), (), s32[]{:S(2)}) async-start(), calls=%async_computation.4 | async-start | bytes 131072 | tf_op jit(solution)/shard_map/psum | solution.py:133
  269.9 143.9 %all-gather.3.cloned.1.call-start = ((), (), s32[]{:S(2)}) async-start(), calls=%async_computation.5 | async-start | bytes 1081344 | tf_op jit(solution)/shard_map/all_gather | solution.py:136
  334.6 311.5 %reduce-scatter.6.cloned.1.call-start = ((), (), s32[]{:S(2)}) async-start(), calls=%async_computation.6 | async-start | bytes 2162688 | tf_op jit(solution)/shard_map/reduce_scatter | solution.py:144
  418.1 0.9 copy-start.3
  418.1 0.9 copy-start.7
  418.1 0.9 copy-start.11
  418.1 1.1 copy-start.4
  429.9 293.4 %all-gather.5.cloned.1.call-start = ((), (), s32[]{:S(2)}) async-start(), calls=%async_computation.7 | async-start | bytes 1081344 | tf_op jit(solution)/shard_map/all_gather | solution.py:151
  647.8 298.1 %reduce-scatter.8.cloned.1.call-start = ((), (), s32[]{:S(2)}) async-start(), calls=%async_computation.8 | async-start | bytes 270336 | tf_op jit(solution)/shard_map/reduce_scatter | solution.py:157
Sparse Core Ops, SparseCore 0:
  48.2 221.6 reduce-scatter.3
  272.2 60.8 all-reduce.1
  336.3 77.4 all-gather.2
  430.0 216.0 reduce-scatter.5
  648.6 74.6 all-gather.4
  732.3 213.5 reduce-scatter.7
where the time goes:
time: 954 us; the launch traced here: 953 us
  waiting for transfers between devices  868 us (91%)
  matrix products  30 us (3%)
  local copies, waits for them, and re-layouts  20.8 us (2%)
  other arithmetic  18.9 us (2%)
  between operations  15.1 us (2%)
    reduce_scatter x1, waiting for transfers between devices, body(): lax.psum_scatter(partial_value, 'dom', scatter_dimension=0, tiled=True)  222 us
    reduce_scatter x1, waiting for transfers between devices, body(): lax.psum_scatter(rows_in_window(flat_contrib, flat_targets, lax.axis_size...  216 us
    reduce_scatter x1, waiting for transfers between devices, body(): lax.psum_scatter(jnp.einsum('bif,bih->fh', aggregated, picked_grads, pref...  214 us
    all_gather x1, waiting for transfers between devices, body(): all_states = lax.all_gather(states, 'dom', axis=0, tiled=True)  77.3 us
    all_gather x1, waiting for transfers between devices, body(): all_grads = lax.all_gather(first_grad, 'dom', axis=0, tiled=True)  75.4 us
    psum x1, waiting for transfers between devices, body(): first = lax.psum(owned, 'cuts')  63.2 us
  transfers between devices with their start and end apart: 6, of which 6 were waited for; matrix products, arithmetic and copies ran while one was open for 0% of the time, Pallas kernels for 0%

commit v1 on v0

--- a/solution.py
+++ b/solution.py
@@ -130,7 +130,9 @@
         projected, blk_dst, num_segments=total_rows // block_rows
     ).reshape(total_rows, hidden)
     owned = lax.psum_scatter(partial_value, "dom", scatter_dimension=0, tiled=True)
-    first = lax.psum(owned, "cuts")
+    first = owned
+    for hop in (1, 2, 4):
+        first = first + lax.ppermute(first, "cuts", [(dev, dev ^ hop) for dev in range(8)])
     state_exact = jnp.tanh(first)
     states = state_exact.astype(jnp.bfloat16)
     all_states = lax.all_gather(states, "dom", axis=0, tiled=True)

time: 954 us -> 897 us (0.940)
  waiting for transfers between devices: 868 us -> 809 us
    psum x1 -> x0, waiting for transfers between devices: 63.2 us -> none  [body(): first = lax.psum(owned, 'cuts')]
  transfers between devices with their start and end apart: 6 -> 8, of which waited for: 6 -> 8; matrix products, arithmetic and copies ran while one was open for 0% -> 0% of each run, Pallas kernels for 0% -> 0%
where the time goes in v1:
time: 897 us
  waiting for transfers between devices  809 us (90%)
  matrix products  30.1 us (3%)
  local copies, waits for them, and re-layouts  20.8 us (2%)
  other arithmetic  19 us (2%)
  between operations  14.7 us (2%)
    reduce_scatter x1, waiting for transfers between devices, body(): lax.psum_scatter(partial_value, 'dom', scatter_dimension=0, tiled=True)  222 us
    reduce_scatter x1, waiting for transfers between devices, body(): lax.psum_scatter(rows_in_window(flat_contrib, flat_targets, lax.axis_size...  216 us
    reduce_scatter x1, waiting for transfers between devices, body(): lax.psum_scatter(jnp.einsum('bif,bih->fh', aggregated, picked_grads, pref...  214 us
    all_gather x1, waiting for transfers between devices, body(): all_grads = lax.all_gather(first_grad, 'dom', axis=0, tiled=True)  75.2 us
    all_gather x1, waiting for transfers between devices, body(): all_states = lax.all_gather(states, 'dom', axis=0, tiled=True)  72.8 us
  transfers between devices with their start and end apart: 8, of which 8 were waited for; matrix products, arithmetic and copies ran while one was open for 0% of the time, Pallas kernels for 0%

profile of v1, /device:TPU:8, one launch (start us, length us, event | category | flops | bytes accessed | tf_op | source)
XLA Modules:
  0.0 896.7 jit_solution(5829891584928711377)
XLA Ops:
  8.6 28.6 %while.12 = (s32[]{:T(128)}, bf16[4,16,128,512]{3,2,1,0:T(8,128)(2,1)}, f32[4,16,128,128]{3,2,1,0:T(8,128)}, bf16[4,16,128,128]{3,2,1,0:T(8,128)(2,1)}, s32[4,16...) while((s32[]{:T(128)}, ...), condition=%wide.region_1.2_spmd, body=%wide.region_0.1_spmd.sunk | while | flops 538182720 | bytes 14817201 | solution.py:119
  8.7 2.3 gather_fusion
  11.0 3.1 bitcast_dynamic-update-slice_fusion.2
  14.1 1.8 fusion.100
  15.9 2.3 gather_fusion
  18.2 3.1 bitcast_dynamic-update-slice_fusion.2
  21.3 1.7 fusion.100
  23.0 2.3 gather_fusion
  25.3 3.1 bitcast_dynamic-update-slice_fusion.2
  28.4 1.7 fusion.100
  30.1 2.3 gather_fusion
  32.4 3.1 bitcast_dynamic-update-slice_fusion.2
  35.5 1.7 fusion.100
  37.9 8.8 scatter_fusion
  46.8 1.3 copy-done.1
  48.2 221.8 %reduce-scatter.4.cloned.1.call-done = f32[128,128]{1,0:T(8,128)} async-done(((f32[4096,128]{1,0:T(8,128)}), f32[128,128]{1,0:T(8,128)}) %reduce-scatter.4.cloned.1.call-update) | async-done | bytes 65552 | tf_op jit(solution)/shard_map/reduce_scatter | solution.py:132
  270.0 1.5 collective-permute-done
  271.5 0.9 add.76
  272.9 3.7 collective-permute-done.1
  276.7 2.2 collective-permute-start.2
  278.9 3.6 collective-permute-done.2
  284.2 0.9 fusion.75
  285.1 72.8 %all-gather.3.cloned.1.call-done = bf16[4096,128]{1,0:T(8,128)(2,1)} async-done(((bf16[128,128]{1,0:T(8,128)(2,1)}), bf16[4096,128]{1,0:T(8,128)(2,1)}) %all-gather.3.cloned.1.call-update) | async-done | bytes 1048592 | tf_op jit(solution)/shard_map/all_gather | solution.py:138
  357.9 4.2 gather_fusion.1
  365.3 7.1 scatter_custom_fusion.1
  372.4 1.5 slice.37
  374.0 216.3 %reduce-scatter.6.cloned.1.call-done = f32[128,128]{1,0:T(8,128)} async-done(((f32[4096,128]{1,0:T(8,128)}), f32[128,128]{1,0:T(8,128)}) %reduce-scatter.6.cloned.1.call-update) | async-done | bytes 65552 | tf_op jit(solution)/shard_map/reduce_scatter | solution.py:146
  590.3 1.6 fusion.61
  592.3 75.2 %all-gather.5.cloned.1.call-done = bf16[4096,128]{1,0:T(8,128)(2,1)} async-done(((bf16[128,128]{1,0:T(8,128)(2,1)}), bf16[4096,128]{1,0:T(8,128)(2,1)}) %all-gather.5.cloned.1.call-update) | async-done | bytes 1048592 | tf_op jit(solution)/shard_map/all_gather | solution.py:153
  667.5 2.2 gather_fusion.2
  669.7 6.7 fusion.12
  676.4 213.7 %reduce-scatter.8.cloned.1.call-done = f32[16,128]{1,0:T(8,128)} async-done(((f32[512,128]{1,0:T(8,128)}), f32[16,128]{1,0:T(8,128)}) %reduce-scatter.8.cloned.1.call-update) | async-done | bytes 8208 | tf_op jit(solution)/shard_map/reduce_scatter | solution.py:159
  (80 shorter events, 7.2 us)
Async XLA Ops:
  7.2 355.7 %copy-start = (bf16[128,384]{1,0:T(8,128)(2,1)S(1)}, bf16[128,384]{1,0:T(8,128)(2,1)}, u32[]{:S(2)}) copy-start(bf16[128,384]{1,0:T(8,128)(2,1)} %param.24) | copy-start | bytes 294916
  7.2 262.8 %reduce-scatter.4.cloned.1.call-start = ((), (), s32[]{:S(2)}) async-start(), calls=%async_computation.3 | async-start | bytes 2162688 | tf_op jit(solution)/shard_map/reduce_scatter | solution.py:132
  10.9 3.1 copy-start.2
  18.2 3.1 copy-start.2
  25.3 3.1 copy-start.2
  32.4 3.1 copy-start.2
  37.3 0.7 copy-start.9
  46.7 1.4 copy-start.1
  46.7 236.5 %copy-start.7 = (s32[128,8]{0,1:T(8,128)S(1)}, s32[128,8]{0,1:T(8,128)}, u32[]{:S(2)}) copy-start(s32[128,8]{0,1:T(8,128)} %param.20) | copy-start | bytes 12292
  46.8 236.7 %copy-start.8 = (s32[128,8]{0,1:T(8,128)S(1)}, s32[128,8]{0,1:T(8,128)}, u32[]{:S(2)}) copy-start(s32[128,8]{0,1:T(8,128)} %param.21) | copy-start | bytes 12292
  46.8 236.8 %copy-start.5 = (bf16[128,512]{1,0:T(8,128)(2,1)S(1)}, bf16[128,512]{1,0:T(8,128)(2,1)}, u32[]{:S(2)}) copy-start(bf16[128,512]{1,0:T(8,128)(2,1)} %param.23) | copy-start | bytes 393220
  46.8 237.4 %copy-start.4 = (bf16[128,256]{1,0:T(8,128)(2,1)S(1)}, bf16[128,256]{1,0:T(8,128)(2,1)}, u32[]{:S(2)}) copy-start(bf16[128,256]{1,0:T(8,128)(2,1)} %param.25) | copy-start | bytes 196612
  48.1 309.8 %all-gather.3.cloned.1.call-start = ((), (), s32[]{:S(2)}) async-start(), calls=%async_computation.4 | async-start | bytes 1081344 | tf_op jit(solution)/shard_map/all_gather | solution.py:138
  270.0 1.5 collective-permute-start
  272.3 4.3 collective-permute-start.1
  276.7 5.9 collective-permute-start.2
  283.2 307.2 %reduce-scatter.6.cloned.1.call-start = ((), (), s32[]{:S(2)}) async-start(), calls=%async_computation.5 | async-start | bytes 2162688 | tf_op jit(solution)/shard_map/reduce_scatter | solution.py:146
  362.2 0.9 copy-start.3
  362.2 0.9 copy-start.6
  362.2 0.9 copy-start.10
  374.0 293.5 %all-gather.5.cloned.1.call-start = ((), (), s32[]{:S(2)}) async-start(), calls=%async_computation.6 | async-start | bytes 1081344 | tf_op jit(solution)/shard_map/all_gather | solution.py:153
  592.0 298.1 %reduce-scatter.8.cloned.1.call-start = ((), (), s32[]{:S(2)}) async-start(), calls=%async_computation.7 | async-start | bytes 270336 | tf_op jit(solution)/shard_map/reduce_scatter | solution.py:159
Sparse Core Ops, SparseCore 0:
  48.2 221.6 reduce-scatter.3
  283.3 74.5 all-gather.2
  374.1 216.2 reduce-scatter.5
  592.8 74.6 all-gather.4
  676.5 213.5 reduce-scatter.7
